TPU v7x, 32 devices: a whole 2x2x4 slice. The times are simulated.
32 devices in a mesh: slab: 8 (over y, x, core), group: 4 (over z).
Axes of the slice: x: 2, y: 2, z: 4, core: 2. Of those that a mesh axis runs over, the one named last changes fastest.
Arguments:
- disp_now: float32 [3, 262144], P(None, 'slab'), may hold values from -6 to 6
- disp_prev: float32 [3, 262144], P(None, 'slab'), may hold values from -6 to 6
- inv_mass: float32 [262144], P('slab'), may hold values from 0.5 to 2
- cell_nodes: int32 [1024, 192], P(('slab', 'group')), may hold values from 0 to 98303
- shape_grads: bfloat16 [1024, 3, 192, 128], P(('slab', 'group')), may hold values from -0.125 to 0.125
- cell_weights: float32 [1024, 128], P(('slab', 'group')), may hold values from 0.5 to 2
- cell_shear: float32 [1024], P(('slab', 'group')), may hold values from 0.5 to 2
- cell_bulk: float32 [1024], P(('slab', 'group')), may hold values from 1 to 4
- block_owner: int32 [1024, 1], P(('slab', 'group')), may hold values from 0 to 7; in each aligned block of 32 rows (0 to 31, 32 to 63, ...) at most 4 rows name the same one
- block_nodes: int32 [1024, 256], P(('slab', 'group')), may hold values from 0 to 32767
- block_phi: float32 [1024, 128, 256], P(('slab', 'group')), may hold values from -0.375 to 0.375
- block_corr: float32 [1024, 128, 128], P(('slab', 'group')), may hold values from -0.5 to 0.5
- block_target: float32 [1024, 3, 128], P(('slab', 'group')), may hold values from -6 to 6
- block_fixed: int32 [1024, 128], P(('slab', 'group')), may hold values 0 or 1
Outputs:
- disp_final: float32 [3, 262144], P(None, 'slab')
Inputs may be any that keep to these rules, and one draw needn't show every extreme that they name: `cell_nodes`: support node numbers run over the slab below, the cell's own slab and the slab above; those outside the head read zero. `block_owner`: among the 32 blocks of one device at most 4 have one owner slab, and in every draw some device has exactly 4 with one owner.
All inputs are finite; a program needn't handle non-finite values. No bound on the sum of `block_fixed` on one device may be relied on, other than what follows from the above.
Results may differ from a plain program's by a relative error of at most 0.0059.
Values may be sent and summed in bfloat16 or wider, within the bound.
No kernel may reach another device: no remote copies, remote signals or barrier semaphores. Data moves between devices by JAX's collectives and lax.ppermute only.
A program may use at most 192 MiB of HBM per device.

v0:
```python
import jax
import jax.numpy as jnp
from jax import lax
from jax.sharding import PartitionSpec as P

CAP = 4


def extended(block, sides, width):
    for axis, dim in sides:
        count = lax.axis_size(axis)
        forward = [(i, i + 1) for i in range(count - 1)]
        backward = [(target, source) for source, target in forward]
        low = lax.ppermute(
            lax.slice_in_dim(block, block.shape[dim] - width, None, axis=dim), axis, forward
        )
        high = lax.ppermute(lax.slice_in_dim(block, 0, width, axis=dim), axis, backward)
        block = jnp.concatenate([low, block, high], axis=dim)
    return block


def from_behind(array, axis, by):
    size = lax.axis_size(axis)
    pairs = [(i, i + by) for i in range(size) if 0 <= i + by < size]
    return lax.ppermute(array, axis, pairs)


def stress_of(grad, shear, bulk):
    identity = jnp.eye(3, dtype=grad.dtype)
    full = grad + identity[None, :, :, None]
    entries = [[full[:, leading, trailing] for trailing in range(3)] for leading in range(3)]
    cofactor = [
        [
            entries[(leading + 1) % 3][(trailing + 1) % 3]
            * entries[(leading + 2) % 3][(trailing + 2) % 3]
            - entries[(leading + 1) % 3][(trailing + 2) % 3]
            * entries[(leading + 2) % 3][(trailing + 1) % 3]
            for trailing in range(3)
        ]
        for leading in range(3)
    ]
    volume = (
        entries[0][0] * cofactor[0][0]
        + entries[0][1] * cofactor[0][1]
        + entries[0][2] * cofactor[0][2]
    )
    clamped = jnp.maximum(volume, 0.3)
    shear_now = shear[:, None]
    factor = (bulk[:, None] * jnp.log(clamped) - shear_now) / clamped
    rows_out = [
        jnp.stack(
            [
                shear_now * entries[leading][trailing] + factor * cofactor[leading][trailing]
                for trailing in range(3)
            ],
            axis=1,
        )
        for leading in range(3)
    ]
    return jnp.stack(rows_out, axis=1)


def body(
    disp_now,
    disp_prev,
    inv_mass,
    cell_nodes,
    shape_grads,
    cell_weights,
    cell_shear,
    cell_bulk,
    block_owner,
    block_nodes,
    block_phi,
    block_corr,
    block_target,
    block_fixed,
):
    width = disp_now.shape[1]
    slabs = lax.axis_size("slab")
    nearby = extended(disp_now.astype(jnp.bfloat16), (("slab", 1),), width)
    gathered = jnp.moveaxis(jnp.take(nearby, cell_nodes, axis=1), 0, 1)
    grad = jnp.einsum("cia,cjap->cijp", gathered, shape_grads, preferred_element_type=jnp.float32)
    stress = stress_of(grad, cell_shear, cell_bulk)
    weighted = (cell_weights[:, None, None, :] * stress).astype(jnp.bfloat16)
    force = jnp.einsum("cijp,cjap->cia", weighted, shape_grads, preferred_element_type=jnp.float32)
    partial_value = (
        jnp.zeros((3, 3 * width), jnp.float32).at[:, cell_nodes].add(jnp.moveaxis(force, 1, 0))
    )
    summed = lax.psum(partial_value, "group")
    from_above = from_behind(summed[:, :width], "slab", -1)
    from_below = from_behind(summed[:, 2 * width :], "slab", 1)
    force_sum = summed[:, width : 2 * width] + from_above + from_below
    disp_next = 2.0 * disp_now - disp_prev - inv_mass[None, :] * force_sum
    support = block_nodes.shape[1]
    owner = block_owner[:, 0]
    matches = (owner[:, None] == jnp.arange(slabs, dtype=jnp.int32)[None, :]).astype(jnp.int32)
    ranked = jnp.sum((jnp.cumsum(matches, axis=0) - matches) * matches, axis=1)
    slot_of = owner * CAP + ranked
    fixed_mask = block_fixed.astype(jnp.float32)
    highest = lax.Precision.HIGHEST
    request = jnp.zeros((slabs * CAP, support), jnp.int32).at[slot_of].set(block_nodes)
    request = request.reshape(slabs, CAP, support)
    asked = lax.all_to_all(request, "slab", split_axis=0, concat_axis=0, tiled=True)
    looked = jnp.moveaxis(jnp.take(disp_next, asked, axis=1), 0, 2)
    returned = lax.all_to_all(looked, "slab", split_axis=0, concat_axis=0, tiled=True)
    returned, asked = (returned, asked)
    values = returned.reshape(slabs * CAP, 3, support)[slot_of]
    interp = jnp.einsum("bma,bia->bim", block_phi, values, precision=highest)
    resid = fixed_mask[:, None, :] * (block_target - interp)
    corr = jnp.einsum("bmq,biq->bim", block_corr, resid, precision=highest)
    delta = jnp.einsum("bma,bim->bia", block_phi, corr, precision=highest)
    outgoing = jnp.zeros((slabs * CAP, 3, support), jnp.float32).at[slot_of].set(delta)
    arrived = lax.all_to_all(
        outgoing.reshape(slabs, CAP, 3, support), "slab", split_axis=0, concat_axis=0, tiled=True
    )
    added = jnp.zeros((3, width), jnp.float32).at[:, asked].add(jnp.moveaxis(arrived, 2, 0))
    return disp_next + lax.psum(added, "group")


def solution(mesh):
    placed = (
        P(None, "slab"),
        P(None, "slab"),
        P("slab"),
        P(("slab", "group"), None),
        P(("slab", "group"), None, None, None),
        P(("slab", "group"), None),
        P(("slab", "group")),
        P(("slab", "group")),
        P(("slab", "group"), None),
        P(("slab", "group"), None),
        P(("slab", "group"), None, None),
        P(("slab", "group"), None, None),
        P(("slab", "group"), None, None),
        P(("slab", "group"), None),
    )
    return jax.shard_map(
        body, mesh=mesh, in_specs=placed, out_specs=P(None, "slab"), check_vma=False
    )
```

profile of v0, /device:TPU:0, one launch (start us, length us, event | category | flops | bytes accessed | tf_op | source)
XLA Modules:
  0.0 435.3 jit_solution(6011149501604761152)
XLA Ops:
  6.5 0.0 copy-start
  6.5 0.0 all-reduce.3.cloned.1.call-start
  6.5 1.3 convert_element_type.19
  7.8 2.4 collective-permute-start
  10.2 1.3 collective-permute-start.1
  11.6 0.8 compare_select_fusion.1
  12.3 0.1 reshape.1417
  12.4 0.8 compare_and_fusion.1
  13.2 0.0 collective-permute-done
  13.2 2.7 collective-permute-done.1
  15.9 1.3 pad_maximum_fusion
  17.2 15.8 %copy.131 = bf16[3,98304]{0,1:T(8,128)(2,1)} copy(bf16[3,98304]{1,0:T(4,128)(2,1)S(1)} %pad_maximum_fusion) | data formatting | bytes 1179648 | tf_op jit(solution)/shard_map/concatenate | solution.py:18
  33.0 32.5 %gather_fusion = bf16[6144,3]{1,0:T(8,128)(2,1)} fusion(bf16[3,98304]{0,1:T(8,128)(2,1)} %copy.131, s32[6144]{0:T(1024)S(1)} %broadcast_clamp_fusion.1), kind=kCustom, calls=%fused_computation | custom fusion | bytes 98304 | tf_op jit(solution)/shard_map/jit(_take)/gather | solution.py:82
  65.5 1.9 copy.132
  67.5 3.3 fusion.10
  70.7 0.1 copy_add_fusion
  70.8 0.0 copy-done.7
  70.8 0.0 copy-done.9
  70.8 0.1 multiply_add_fusion.8
  70.9 0.1 multiply_add_fusion.7
  71.0 0.1 multiply_add_fusion.6
  71.1 0.0 copy-done.6
  71.1 4.1 convolution_bitcast_fusion
  75.2 2.2 copy.149
  77.4 53.3 %scatter_custom_fusion = f32[3,98304]{0,1:T(8,128)} fusion(s32[6144]{0:T(1024)S(1)} %reshape.1417, f32[6144,3]{1,0:T(8,128)} %bitcast.170, f32[]{:T(128)} %constant.16.clone.1), kind=kCustom, calls=%fused_computation.7 | custom fusion | flops 18432 | bytes 1180160 | tf_op jit(solution)/shard_map/scatter-add | solution.py:88
  130.7 26.7 %copy.137 = f32[3,98304]{1,0:T(4,128)} copy(f32[3,98304]{0,1:T(8,128)} %scatter_custom_fusion) | data formatting | bytes 2359296 | tf_op jit(solution)/shard_map/scatter-add | solution.py:88
  157.4 0.0 all-reduce.3.cloned.1.call-update
  157.4 0.0 copy-done.8
  157.4 0.1 fusion.16
  157.5 0.1 reduce_window_sum.11
  157.5 0.2 select_reduce_fusion
  157.7 0.9 scatter_custom_fusion.1
  158.7 0.6 reshape.1388
  159.3 8.0 %all-to-all-start = ((s32[8,4,256]{2,1,0:T(4,128)}), s32[8,4,256]{2,1,0:T(4,128)S(1)}, u32[]{:S(2)}, u32[]{:S(2)}) async-start(s32[8,4,256]{2,1,0:T(4,128)} %reshape.1388), calls=%async_computation | async-start | bytes 65536 | tf_op jit(solution)/shard_map/all_to_all | solution.py:104
  167.3 0.0 copy-done.5
  167.3 4.8 %all-to-all-done = s32[8,4,256]{2,1,0:T(4,128)S(1)} async-done(((s32[8,4,256]{2,1,0:T(4,128)}), s32[8,4,256]{2,1,0:T(4,128)S(1)}, u32[]{:S(2)}, u32[]{:S(2)}) %all-to-all-start) | async-done | bytes 32800 | tf_op jit(solution)/shard_map/all_to_all | solution.py:104
  172.2 59.9 %all-reduce.3.cloned.1.call-done = f32[3,98304]{1,0:T(4,128)} async-done(((f32[3,98304]{1,0:T(4,128)}), f32[3,98304]{1,0:T(4,128)}) %all-reduce.3.cloned.1.call-update) | async-done | bytes 1179664 | tf_op jit(solution)/shard_map/psum | solution.py:90
  232.1 1.4 fusion.22
  233.5 1.3 collective-permute-start.2
  234.8 3.1 collective-permute-start.3
  237.9 0.0 collective-permute-done.2
  237.9 1.4 collective-permute-done.3
  239.4 0.0 copy-done.3
  239.4 1.6 fusion.7
  240.9 8.6 %copy.138 = f32[3,32768]{0,1:T(8,128)} copy(f32[3,32768]{1,0:T(4,128)S(1)} %fusion.7) | data formatting | bytes 786432 | tf_op jit(solution)/shard_map/sub | solution.py:94
  249.5 33.5 %gather_fusion.1 = f32[8192,3]{1,0:T(8,128)} fusion(f32[3,32768]{0,1:T(8,128)} %copy.138, s32[8192]{0:T(1024)S(1)} %broadcast_clamp_fusion), kind=kCustom, calls=%fused_computation.1 | custom fusion | bytes 229376 | tf_op jit(solution)/shard_map/jit(_take)/gather | solution.py:105
  283.0 2.8 copy.139
  285.8 0.7 select_bitcast_fusion
  286.5 13.2 %all-to-all-start.1 = ((f32[8,4,3,256]{3,1,2,0:T(4,128)}), f32[8,4,3,256]{3,1,2,0:T(4,128)S(1)}, u32[]{:S(2)}, u32[]{:S(2)}) async-start(f32[8,4,3,256]{3,1,2,0:T(4,128)} %select_bitcast_fusion), calls=%async_computation.1 | async-start | bytes 196608 | tf_op jit(solution)/shard_map/all_to_all | solution.py:106
  299.6 0.0 all-reduce.5.cloned.1.call-start
  299.7 5.1 %all-to-all-done.1 = f32[8,4,3,256]{3,1,2,0:T(4,128)S(1)} async-done(((f32[8,4,3,256]{3,1,2,0:T(4,128)}), f32[8,4,3,256]{3,1,2,0:T(4,128)S(1)}, u32[]{:S(2)}, u32[]{:S(2)}) %all-to-all-start.1) | async-done | bytes 98336 | tf_op jit(solution)/shard_map/all_to_all | solution.py:106
  304.9 0.6 gather_fusion.2
  305.5 0.0 copy-start.1
  305.5 5.8 %fusion.4 = f32[32,3,128]{2,1,0:T(4,128)S(1)} fusion(f32[32,3,256]{2,1,0:T(4,128)S(1)} %gather_fusion.2, f32[32,128,256]{2,1,0:T(8,128)} %param.24, f32[32,3,128]{2,0,1:T(8,128)S(1)} %copy-done.4, f32[32,128]{1,0:T(8,128)S(1)} %convert_element_type.23), kind=kOutput, calls=%fused_computation.13 | convolution fusion | flops 37773312 | bytes 4407296 | tf_op jit(solution)/shard_map/bma,bia->bim/dot_general | solution.py:109
  311.4 3.4 fusion.23
  314.7 2.1 fusion.24
  316.9 1.5 scatter_fusion
  318.4 7.6 %all_to_all.15 = f32[8,4,3,256]{3,1,2,0:T(4,128)S(1)} all-to-all(f32[8,4,3,256]{3,1,2,0:T(4,128)S(1)} %copy.143), channel_id=1, replica_groups=mesh['slab'=8,'group'=4] {'slab'}, dimensions={0} | all-to-all | bytes 196608 | tf_op jit(solution)/shard_map/all_to_all | solution.py:114
  326.0 2.6 copy.151
  328.6 51.1 %scatter_custom_fusion.3 = f32[3,32768]{0,1:T(8,128)} fusion(s32[8192]{0:T(1024)S(1)} %bitcast.176, f32[8192,3]{1,0:T(8,128)} %bitcast.169, f32[]{:T(128)} %constant.16.clone.1), kind=kCustom, calls=%fused_computation.9 | custom fusion | flops 24576 | bytes 393728 | tf_op jit(solution)/shard_map/scatter-add | solution.py:117
  379.7 9.8 %copy.146 = f32[3,32768]{1,0:T(4,128)} copy(f32[3,32768]{0,1:T(8,128)} %scatter_custom_fusion.3) | data formatting | bytes 786432 | tf_op jit(solution)/shard_map/scatter-add | solution.py:117
  389.5 0.0 all-reduce.5.cloned.1.call-update
  389.5 37.0 %all-reduce.5.cloned.1.call-done = f32[3,32768]{1,0:T(4,128)} async-done(((f32[3,32768]{1,0:T(4,128)}), f32[3,32768]{1,0:T(4,128)}) %all-reduce.5.cloned.1.call-update) | async-done | bytes 393232 | tf_op jit(solution)/shard_map/psum | solution.py:118
  426.5 2.0 add.250
  (27 shorter events, 0.2 us)
Async XLA Ops:
  6.5 304.8 %copy-start = (f32[32,128,128]{2,1,0:T(8,128)S(1)}, f32[32,128,128]{2,1,0:T(8,128)}, u32[]{:S(2)}) copy-start(f32[32,128,128]{2,1,0:T(8,128)} %param.25) | copy-start | bytes 6291460
  6.5 225.6 %all-reduce.3.cloned.1.call-start = ((), (), s32[]{:S(2)}) async-start(), calls=%async_computation.3 | async-start | bytes 3145728 | tf_op jit(solution)/shard_map/psum | solution.py:90
  7.8 5.4 %collective-permute-start = (bf16[3,32768]{1,0:T(4,128)(2,1)S(1)}, bf16[3,32768]{1,0:T(4,128)(2,1)S(1)}, u32[]{:S(2)}, u32[]{:S(2)}) collective-permute-start(bf16[3,32768]{1,0:T(4,128)(2,1)S(1)} %convert_element_type.19), channel_id=1, source_target_pairs={{0,4},{4,8},{8,12},{12,16},{16,20},{20,24},{24,28},{1,5},{5,9},{9,... | collective-permute-start | bytes 589832 | tf_op jit(solution)/shard_map/ppermute | solution.py:14
  10.2 5.6 %collective-permute-start.1 = (bf16[3,32768]{1,0:T(4,128)(2,1)S(1)}, bf16[3,32768]{1,0:T(4,128)(2,1)}, u32[]{:S(2)}, u32[]{:S(2)}) collective-permute-start(bf16[3,32768]{1,0:T(4,128)(2,1)S(1)} %convert_element_type.19), channel_id=1, source_target_pairs={{4,0},{8,4},{12,8},{16,12},{20,16},{24,20},{28,24},{5,1},{9,5},{13... | collective-permute-start | bytes 589832 | tf_op jit(solution)/shard_map/ppermute | solution.py:17
  33.0 37.8 %copy-start.7 = (f32[32]{0:T(128)S(1)}, f32[32]{0:T(128)}, u32[]{:S(2)}) copy-start(f32[32]{0:T(128)} %param.20) | copy-start | bytes 388
  33.0 37.8 %copy-start.9 = (f32[32]{0:T(128)S(1)}, f32[32]{0:T(128)}, u32[]{:S(2)}) copy-start(f32[32]{0:T(128)} %param.21) | copy-start | bytes 388
  33.0 38.1 %copy-start.6 = (f32[32,128]{1,0:T(8,128)S(1)}, f32[32,128]{1,0:T(8,128)}, u32[]{:S(2)}) copy-start(f32[32,128]{1,0:T(8,128)} %param.19) | copy-start | bytes 49156
  130.7 26.7 %copy-start.8 = (s32[32,1]{0,1:T(1,128)S(1)}, s32[32,1]{0,1:T(1,128)}, u32[]{:S(2)}) copy-start(s32[32,1]{0,1:T(1,128)} %param.22) | copy-start | bytes 388
  130.7 36.6 %copy-start.5 = (s32[32,128]{1,0:T(8,128)S(1)}, s32[32,128]{1,0:T(8,128)}, u32[]{:S(2)}) copy-start(s32[32,128]{1,0:T(8,128)} %param.27) | copy-start | bytes 49156
  157.4 82.0 %copy-start.2 = (f32[3,32768]{1,0:T(4,128)S(1)}, f32[3,32768]{1,0:T(4,128)}, u32[]{:S(2)}) copy-start(f32[3,32768]{1,0:T(4,128)} %param.14) | copy-start | bytes 1179652
  157.4 82.0 %copy-start.3 = (f32[32768]{0:T(1024)S(1)}, f32[32768]{0:T(1024)}, u32[]{:S(2)}) copy-start(f32[32768]{0:T(1024)} %param.16) | copy-start | bytes 393220
  159.3 12.8 %all-to-all-start = ((s32[8,4,256]{2,1,0:T(4,128)}), s32[8,4,256]{2,1,0:T(4,128)S(1)}, u32[]{:S(2)}, u32[]{:S(2)}) async-start(s32[8,4,256]{2,1,0:T(4,128)} %reshape.1388), calls=%async_computation | async-start | bytes 65536 | tf_op jit(solution)/shard_map/all_to_all | solution.py:104
  233.5 4.4 %collective-permute-start.2 = (f32[3,32768]{1,0:T(4,128)S(1)}, f32[3,32768]{1,0:T(4,128)S(1)}, u32[]{:S(2)}, u32[]{:S(2)}) collective-permute-start(f32[3,32768]{1,0:T(4,128)S(1)} %get-tuple-element.9), channel_id=1, source_target_pairs={{4,0},{8,4},{12,8},{16,12},{20,16},{24,20},{28,24},{5,1},{9,5},{13... | collective-permute-start | bytes 1179656 | tf_op jit(solution)/shard_map/ppermute | solution.py:25
  234.8 4.6 %collective-permute-start.3 = (f32[3,32768]{1,0:T(4,128)S(1)}, f32[3,32768]{1,0:T(4,128)S(1)}, u32[]{:S(2)}, u32[]{:S(2)}) collective-permute-start(f32[3,32768]{1,0:T(4,128)S(1)} %get-tuple-element.10), channel_id=1, source_target_pairs={{0,4},{4,8},{8,12},{12,16},{16,20},{20,24},{24,28},{1,5},{5,9},{9,... | collective-permute-start | bytes 1179656 | tf_op jit(solution)/shard_map/ppermute | solution.py:25
  249.5 56.0 %copy-start.4 = (f32[32,3,128]{2,0,1:T(8,128)S(1)}, f32[32,3,128]{2,0,1:T(8,128)}, u32[]{:S(2)}) copy-start(f32[32,3,128]{2,0,1:T(8,128)} %param.26) | copy-start | bytes 147460
  286.5 18.4 %all-to-all-start.1 = ((f32[8,4,3,256]{3,1,2,0:T(4,128)}), f32[8,4,3,256]{3,1,2,0:T(4,128)S(1)}, u32[]{:S(2)}, u32[]{:S(2)}) async-start(f32[8,4,3,256]{3,1,2,0:T(4,128)} %select_bitcast_fusion), calls=%async_computation.1 | async-start | bytes 196608 | tf_op jit(solution)/shard_map/all_to_all | solution.py:106
  299.6 126.9 %all-reduce.5.cloned.1.call-start = ((), (), s32[]{:S(2)}) async-start(), calls=%async_computation.4 | async-start | bytes 1048576 | tf_op jit(solution)/shard_map/psum | solution.py:118
  305.5 9.2 %copy-start.1 = (f32[32,128,256]{2,1,0:T(8,128)S(1)}, f32[32,128,256]{2,1,0:T(8,128)}, u32[]{:S(2)}) copy-start(f32[32,128,256]{2,1,0:T(8,128)} %param.24) | copy-start | bytes 12582916
Sparse Core Ops, SparseCore 0:
  157.5 74.5 all-reduce.2
  389.6 36.8 all-reduce.4
where the time goes:
time: 437 us; the launch traced here: 435 us
  local copies, waits for them, and re-layouts  142 us (32%)
  other arithmetic  113 us (26%)
  waiting for transfers between devices  111 us (25%)
  starting transfers between devices  29.3 us (7%)
  matrix products  18.6 us (4%)
  between operations  13.7 us (3%)
  blocking collectives  7.58 us (2%)
    psum x1, waiting for transfers between devices, body(): summed = lax.psum(partial_value, 'group')  59.9 us
    scatter-add x1, other arithmetic, body(): jnp.zeros((3, 3 * width), jnp.float32).at[:, cell_nodes]  53.3 us
    scatter-add x1, other arithmetic, body(): jnp.zeros((3, width), jnp.float32).at[:, asked]  51.1 us
    psum x1, waiting for transfers between devices, body(): return disp_next + lax.psum(added, 'group')  37 us
    gather x2, local copies, waits for them, and re-layouts, body(): looked = jnp.moveaxis(jnp.take(disp_next, asked, axis=1), 0, 2)  36.3 us
    gather x2, local copies, waits for them, and re-layouts, body(): gathered = jnp.moveaxis(jnp.take(nearby, cell_nodes, axis=1), 0, 1)  34.5 us
    scatter-add x1, local copies, waits for them, and re-layouts, body(): jnp.zeros((3, 3 * width), jnp.float32).at[:, cell_nodes]  26.7 us
    concatenate x1, local copies, waits for them, and re-layouts, extended(): block = jnp.concatenate([low, block, high], axis=dim)  15.8 us
  transfers between devices with their start and end apart: 8, of which 6 were waited for; matrix products, arithmetic and copies ran while one was open for 1% of the time, Pallas kernels for 0%

commit v1 on v0

--- a/solution.py
+++ b/solution.py
@@ -1,9 +1,21 @@
+import functools
 import jax
 import jax.numpy as jnp
 from jax import lax
 from jax.sharding import PartitionSpec as P
 
 CAP = 4
+
+
+def ratios_meet(incoming_x, across):
+    k_all = lax.axis_size(across)
+    out_arr = incoming_x
+    for dd in [[(c, c ^ s) for c in range(k_all)] for s in (1, 2, 4, 8, 16) if s < k_all]:
+        out_arr = out_arr + lax.ppermute(out_arr, axis_name=across, perm=dd)
+    return out_arr
+
+
+sectors_prepare = functools.partial(ratios_meet, across="group")
 
 
 def extended(block, sides, width):
@@ -87,7 +99,7 @@
     partial_value = (
         jnp.zeros((3, 3 * width), jnp.float32).at[:, cell_nodes].add(jnp.moveaxis(force, 1, 0))
     )
-    summed = lax.psum(partial_value, "group")
+    summed = sectors_prepare(partial_value)
     from_above = from_behind(summed[:, :width], "slab", -1)
     from_below = from_behind(summed[:, 2 * width :], "slab", 1)
     force_sum = summed[:, width : 2 * width] + from_above + from_below

time: 437 us -> 479 us (1.096)
  waiting for transfers between devices: 111 us -> 135 us
  starting transfers between devices: 29.3 us -> 43.7 us
  other arithmetic: 113 us -> 118 us
    ppermute x0 -> x2, waiting for transfers between devices: none -> 83.5 us  [ratios_meet(): out_arr = out_arr + lax.ppermute(out_arr, axis_name=across, perm=dd)]
    psum x1 -> x0, waiting for transfers between devices: 59.9 us -> none  [body(): summed = lax.psum(partial_value, 'group')]
    all_to_all x1, starting transfers between devices: 13.2 us -> 20.5 us  [body(): lax.all_to_all(looked, 'slab', split_axis=0, concat_axis=0, tiled=True)]
    add x0 -> x2, other arithmetic: none -> 5.23 us  [ratios_meet(): out_arr = out_arr + lax.ppermute(out_arr, axis_name=across, perm=dd)]
  transfers between devices with their start and end apart: 8 -> 9, of which waited for: 6 -> 7; matrix products, arithmetic and copies ran while one was open for 1% -> 1% of each run, Pallas kernels for 0% -> 0%
where the time goes in v1:
time: 479 us; the launch traced here: 478 us
  local copies, waits for them, and re-layouts  141 us (29%)
  waiting for transfers between devices  135 us (28%)
  other arithmetic  118 us (25%)
  starting transfers between devices  43.7 us (9%)
  matrix products  18.6 us (4%)
  between operations  13.7 us (3%)
  blocking collectives  7.58 us (2%)
    ppermute x2, waiting for transfers between devices, ratios_meet(): out_arr = out_arr + lax.ppermute(out_arr, axis_name=across, perm=dd)  83.5 us
    scatter-add x1, other arithmetic, body(): jnp.zeros((3, 3 * width), jnp.float32).at[:, cell_nodes]  53.3 us
    scatter-add x1, other arithmetic, body(): jnp.zeros((3, width), jnp.float32).at[:, asked]  51.1 us
    psum x1, waiting for transfers between devices, body(): return disp_next + lax.psum(added, 'group')  38.1 us
    gather x2, local copies, waits for them, and re-layouts, body(): looked = jnp.moveaxis(jnp.take(disp_next, asked, axis=1), 0, 2)  36.4 us
    gather x2, local copies, waits for them, and re-layouts, body(): gathered = jnp.moveaxis(jnp.take(nearby, cell_nodes, axis=1), 0, 1)  34.5 us
    scatter-add x1, local copies, waits for them, and re-layouts, body(): jnp.zeros((3, 3 * width), jnp.float32).at[:, cell_nodes]  26.7 us
    all_to_all x1, starting transfers between devices, body(): lax.all_to_all(looked, 'slab', split_axis=0, concat_axis=0, tiled=True)  20.5 us
  transfers between devices with their start and end apart: 9, of which 7 were waited for; matrix products, arithmetic and copies ran while one was open for 1% of the time, Pallas kernels for 0%

profile of v1, /device:TPU:0, one launch (start us, length us, event | category | flops | bytes accessed | tf_op | source)
XLA Modules:
  0.0 478.1 jit_solution(6914125431201260819)
XLA Ops:
  6.5 0.0 copy-start
  6.5 1.3 convert_element_type.19
  7.8 2.4 collective-permute-start
  10.2 1.3 collective-permute-start.1
  11.6 0.8 compare_select_fusion.1
  12.3 0.1 reshape.1417
  12.4 0.8 compare_and_fusion.1
  13.2 0.0 collective-permute-done
  13.2 2.7 collective-permute-done.1
  15.9 1.3 pad_maximum_fusion
  17.2 15.8 %copy.143 = bf16[3,98304]{0,1:T(8,128)(2,1)} copy(bf16[3,98304]{1,0:T(4,128)(2,1)S(1)} %pad_maximum_fusion) | data formatting | bytes 1179648 | tf_op jit(solution)/shard_map/concatenate | solution.py:30
  33.0 32.5 %gather_fusion = bf16[6144,3]{1,0:T(8,128)(2,1)} fusion(bf16[3,98304]{0,1:T(8,128)(2,1)} %copy.143, s32[6144]{0:T(1024)S(1)} %broadcast_clamp_fusion.1), kind=kCustom, calls=%fused_computation | custom fusion | bytes 98304 | tf_op jit(solution)/shard_map/jit(_take)/gather | solution.py:94
  65.6 1.9 copy.144
  67.5 3.3 fusion.10
  70.8 0.1 copy_add_fusion
  70.9 0.0 copy-done.7
  70.9 0.0 copy-done.9
  70.9 0.1 multiply_add_fusion.8
  71.0 0.1 multiply_add_fusion.7
  71.0 0.1 multiply_add_fusion.6
  71.1 0.0 copy-done.6
  71.2 4.1 convolution_bitcast_fusion
  75.2 2.2 copy.162
  77.5 53.3 %scatter_custom_fusion = f32[3,98304]{0,1:T(8,128)} fusion(s32[6144]{0:T(1024)S(1)} %reshape.1417, f32[6144,3]{1,0:T(8,128)} %bitcast.170, f32[]{:T(128)} %constant.16.clone.1), kind=kCustom, calls=%fused_computation.7 | custom fusion | flops 18432 | bytes 1180160 | tf_op jit(solution)/shard_map/scatter-add | solution.py:100
  130.7 26.7 %copy.150 = f32[3,98304]{1,0:T(4,128)} copy(f32[3,98304]{0,1:T(8,128)} %scatter_custom_fusion) | data formatting | bytes 2359296 | tf_op jit(solution)/shard_map/scatter-add | solution.py:100
  157.4 1.6 collective-permute-start.2
  158.9 32.1 %collective-permute-done.2 = f32[3,98304]{1,0:T(4,128)S(1)} collective-permute-done((f32[3,98304]{1,0:T(4,128)}, f32[3,98304]{1,0:T(4,128)S(1)}, u32[]{:S(2)}, u32[]{:S(2)}) %collective-permute-start.2) | collective-permute-done | bytes 1179680 | tf_op jit(solution)/shard_map/ppermute | solution.py:14
  191.0 2.9 add.248
  194.0 2.6 collective-permute-start.3
  196.6 0.1 fusion.16
  196.6 0.1 reduce_window_sum.11
  196.7 0.2 select_reduce_fusion
  196.9 0.9 scatter_custom_fusion.1
  197.8 0.6 reshape.1388
  198.5 10.4 %all-to-all-start = ((s32[8,4,256]{2,1,0:T(4,128)}), s32[8,4,256]{2,1,0:T(4,128)S(1)}, u32[]{:S(2)}, u32[]{:S(2)}) async-start(s32[8,4,256]{2,1,0:T(4,128)} %reshape.1388), calls=%async_computation | async-start | bytes 65536 | tf_op jit(solution)/shard_map/all_to_all | solution.py:116
  208.9 4.8 %all-to-all-done = s32[8,4,256]{2,1,0:T(4,128)S(1)} async-done(((s32[8,4,256]{2,1,0:T(4,128)}), s32[8,4,256]{2,1,0:T(4,128)S(1)}, u32[]{:S(2)}, u32[]{:S(2)}) %all-to-all-start) | async-done | bytes 32800 | tf_op jit(solution)/shard_map/all_to_all | solution.py:116
  213.7 51.4 %collective-permute-done.3 = f32[3,98304]{1,0:T(4,128)} collective-permute-done((f32[3,98304]{1,0:T(4,128)}, f32[3,98304]{1,0:T(4,128)}, u32[]{:S(2)}, u32[]{:S(2)}) %collective-permute-start.3) | collective-permute-done | bytes 1179680 | tf_op jit(solution)/shard_map/ppermute | solution.py:14
  265.1 2.3 add.249
  267.4 0.2 fusion.22
  267.6 1.3 collective-permute-start.4
  268.9 3.5 collective-permute-start.5
  272.4 0.0 collective-permute-done.4
  272.4 1.4 collective-permute-done.5
  273.8 1.4 fusion.7
  275.3 8.6 %copy.151 = f32[3,32768]{0,1:T(8,128)} copy(f32[3,32768]{1,0:T(4,128)S(1)} %fusion.7) | data formatting | bytes 786432 | tf_op jit(solution)/shard_map/sub | solution.py:106
  283.8 33.5 %gather_fusion.1 = f32[8192,3]{1,0:T(8,128)} fusion(f32[3,32768]{0,1:T(8,128)} %copy.151, s32[8192]{0:T(1024)S(1)} %broadcast_clamp_fusion), kind=kCustom, calls=%fused_computation.1 | custom fusion | bytes 229376 | tf_op jit(solution)/shard_map/jit(_take)/gather | solution.py:117
  317.3 2.8 copy.152
  320.2 0.7 select_bitcast_fusion
  320.9 20.5 %all-to-all-start.1 = ((f32[8,4,3,256]{3,1,2,0:T(4,128)}), f32[8,4,3,256]{3,1,2,0:T(4,128)S(1)}, u32[]{:S(2)}, u32[]{:S(2)}) async-start(f32[8,4,3,256]{3,1,2,0:T(4,128)} %select_bitcast_fusion), calls=%async_computation.1 | async-start | bytes 196608 | tf_op jit(solution)/shard_map/all_to_all | solution.py:118
  341.3 0.3 all-reduce.2.cloned.1.call-start
  341.6 4.9 %all-to-all-done.1 = f32[8,4,3,256]{3,1,2,0:T(4,128)S(1)} async-done(((f32[8,4,3,256]{3,1,2,0:T(4,128)}), f32[8,4,3,256]{3,1,2,0:T(4,128)S(1)}, u32[]{:S(2)}, u32[]{:S(2)}) %all-to-all-start.1) | async-done | bytes 98336 | tf_op jit(solution)/shard_map/all_to_all | solution.py:118
  346.6 0.6 gather_fusion.2
  347.2 0.0 copy-start.1
  347.2 5.8 %fusion.4 = f32[32,3,128]{2,1,0:T(4,128)S(1)} fusion(f32[32,3,256]{2,1,0:T(4,128)S(1)} %gather_fusion.2, f32[32,128,256]{2,1,0:T(8,128)} %param.24, f32[32,3,128]{2,0,1:T(8,128)S(1)} %copy-done.4, f32[32,128]{1,0:T(8,128)S(1)} %convert_element_type.23), kind=kOutput, calls=%fused_computation.13 | convolution fusion | flops 37773312 | bytes 4407296 | tf_op jit(solution)/shard_map/bma,bia->bim/dot_general | solution.py:121
  353.1 3.4 fusion.23
  356.4 2.1 fusion.24
  358.6 1.5 scatter_fusion
  360.1 7.6 %all_to_all.15 = f32[8,4,3,256]{3,1,2,0:T(4,128)S(1)} all-to-all(f32[8,4,3,256]{3,1,2,0:T(4,128)S(1)} %copy.156), channel_id=1, replica_groups=mesh['slab'=8,'group'=4] {'slab'}, dimensions={0} | all-to-all | bytes 196608 | tf_op jit(solution)/shard_map/all_to_all | solution.py:126
  367.7 2.6 copy.164
  370.3 51.1 %scatter_custom_fusion.3 = f32[3,32768]{0,1:T(8,128)} fusion(s32[8192]{0:T(1024)S(1)} %bitcast.176, f32[8192,3]{1,0:T(8,128)} %bitcast.169, f32[]{:T(128)} %constant.16.clone.1), kind=kCustom, calls=%fused_computation.9 | custom fusion | flops 24576 | bytes 393728 | tf_op jit(solution)/shard_map/scatter-add | solution.py:129
  421.3 9.8 %copy.159 = f32[3,32768]{1,0:T(4,128)} copy(f32[3,32768]{0,1:T(8,128)} %scatter_custom_fusion.3) | data formatting | bytes 786432 | tf_op jit(solution)/shard_map/scatter-add | solution.py:129
  431.2 0.0 all-reduce.2.cloned.1.call-update
  431.2 38.1 %all-reduce.2.cloned.1.call-done = f32[3,32768]{1,0:T(4,128)} async-done(((f32[3,32768]{1,0:T(4,128)}), f32[3,32768]{1,0:T(4,128)}) %all-reduce.2.cloned.1.call-update) | async-done | bytes 393232 | tf_op jit(solution)/shard_map/psum | solution.py:130
  469.3 2.0 add.256
  (30 shorter events, 0.2 us)
Async XLA Ops:
  6.5 346.5 %copy-start = (f32[32,128,128]{2,1,0:T(8,128)S(1)}, f32[32,128,128]{2,1,0:T(8,128)}, u32[]{:S(2)}) copy-start(f32[32,128,128]{2,1,0:T(8,128)} %param.25) | copy-start | bytes 6291460
  7.8 5.4 %collective-permute-start = (bf16[3,32768]{1,0:T(4,128)(2,1)S(1)}, bf16[3,32768]{1,0:T(4,128)(2,1)S(1)}, u32[]{:S(2)}, u32[]{:S(2)}) collective-permute-start(bf16[3,32768]{1,0:T(4,128)(2,1)S(1)} %convert_element_type.19), channel_id=1, source_target_pairs={{0,4},{4,8},{8,12},{12,16},{16,20},{20,24},{24,28},{1,5},{5,9},{9,... | collective-permute-start | bytes 589832 | tf_op jit(solution)/shard_map/ppermute | solution.py:26
  10.2 5.6 %collective-permute-start.1 = (bf16[3,32768]{1,0:T(4,128)(2,1)S(1)}, bf16[3,32768]{1,0:T(4,128)(2,1)}, u32[]{:S(2)}, u32[]{:S(2)}) collective-permute-start(bf16[3,32768]{1,0:T(4,128)(2,1)S(1)} %convert_element_type.19), channel_id=1, source_target_pairs={{4,0},{8,4},{12,8},{16,12},{20,16},{24,20},{28,24},{5,1},{9,5},{13... | collective-permute-start | bytes 589832 | tf_op jit(solution)/shard_map/ppermute | solution.py:29
  33.0 37.8 %copy-start.7 = (f32[32]{0:T(128)S(1)}, f32[32]{0:T(128)}, u32[]{:S(2)}) copy-start(f32[32]{0:T(128)} %param.20) | copy-start | bytes 388
  33.0 37.8 %copy-start.9 = (f32[32]{0:T(128)S(1)}, f32[32]{0:T(128)}, u32[]{:S(2)}) copy-start(f32[32]{0:T(128)} %param.21) | copy-start | bytes 388
  33.0 38.1 %copy-start.6 = (f32[32,128]{1,0:T(8,128)S(1)}, f32[32,128]{1,0:T(8,128)}, u32[]{:S(2)}) copy-start(f32[32,128]{1,0:T(8,128)} %param.19) | copy-start | bytes 49156
  157.4 39.2 %copy-start.8 = (s32[32,1]{0,1:T(1,128)S(1)}, s32[32,1]{0,1:T(1,128)}, u32[]{:S(2)}) copy-start(s32[32,1]{0,1:T(1,128)} %param.22) | copy-start | bytes 388
  157.4 51.5 %copy-start.5 = (s32[32,128]{1,0:T(8,128)S(1)}, s32[32,128]{1,0:T(8,128)}, u32[]{:S(2)}) copy-start(s32[32,128]{1,0:T(8,128)} %param.27) | copy-start | bytes 49156
  157.4 33.7 %collective-permute-start.2 = (f32[3,98304]{1,0:T(4,128)}, f32[3,98304]{1,0:T(4,128)S(1)}, u32[]{:S(2)}, u32[]{:S(2)}) collective-permute-start(f32[3,98304]{1,0:T(4,128)} %copy.150), channel_id=1, source_target_pairs={{0,1},{1,0},{2,3},{3,2},{4,5},{5,4},{6,7},{7,6},{8,9},{9,8},{10,11... | collective-permute-start | bytes 3538952 | tf_op jit(solution)/shard_map/ppermute | solution.py:14
  194.0 79.9 %copy-start.2 = (f32[3,32768]{1,0:T(4,128)S(1)}, f32[3,32768]{1,0:T(4,128)}, u32[]{:S(2)}) copy-start(f32[3,32768]{1,0:T(4,128)} %param.14) | copy-start | bytes 1179652
  194.0 79.9 %copy-start.3 = (f32[32768]{0:T(1024)S(1)}, f32[32768]{0:T(1024)}, u32[]{:S(2)}) copy-start(f32[32768]{0:T(1024)} %param.16) | copy-start | bytes 393220
  194.0 71.1 %collective-permute-start.3 = (f32[3,98304]{1,0:T(4,128)}, f32[3,98304]{1,0:T(4,128)}, u32[]{:S(2)}, u32[]{:S(2)}) collective-permute-start(f32[3,98304]{1,0:T(4,128)} %add.248), channel_id=1, source_target_pairs={{0,2},{1,3},{2,0},{3,1},{4,6},{5,7},{6,4},{7,5},{8,10},{9,11},{10,... | collective-permute-start | bytes 3538952 | tf_op jit(solution)/shard_map/ppermute | solution.py:14
  198.5 15.2 %all-to-all-start = ((s32[8,4,256]{2,1,0:T(4,128)}), s32[8,4,256]{2,1,0:T(4,128)S(1)}, u32[]{:S(2)}, u32[]{:S(2)}) async-start(s32[8,4,256]{2,1,0:T(4,128)} %reshape.1388), calls=%async_computation | async-start | bytes 65536 | tf_op jit(solution)/shard_map/all_to_all | solution.py:116
  267.6 4.8 %collective-permute-start.4 = (f32[3,32768]{1,0:T(4,128)S(1)}, f32[3,32768]{1,0:T(4,128)S(1)}, u32[]{:S(2)}, u32[]{:S(2)}) collective-permute-start(f32[3,32768]{1,0:T(4,128)S(1)} %get-tuple-element.9), channel_id=1, source_target_pairs={{4,0},{8,4},{12,8},{16,12},{20,16},{24,20},{28,24},{5,1},{9,5},{13... | collective-permute-start | bytes 1179656 | tf_op jit(solution)/shard_map/ppermute | solution.py:37
  268.9 5.0 %collective-permute-start.5 = (f32[3,32768]{1,0:T(4,128)S(1)}, f32[3,32768]{1,0:T(4,128)S(1)}, u32[]{:S(2)}, u32[]{:S(2)}) collective-permute-start(f32[3,32768]{1,0:T(4,128)S(1)} %get-tuple-element.10), channel_id=1, source_target_pairs={{0,4},{4,8},{8,12},{12,16},{16,20},{20,24},{24,28},{1,5},{5,9},{9,... | collective-permute-start | bytes 1179656 | tf_op jit(solution)/shard_map/ppermute | solution.py:37
  283.8 63.4 %copy-start.4 = (f32[32,3,128]{2,0,1:T(8,128)S(1)}, f32[32,3,128]{2,0,1:T(8,128)}, u32[]{:S(2)}) copy-start(f32[32,3,128]{2,0,1:T(8,128)} %param.26) | copy-start | bytes 147460
  320.9 25.7 %all-to-all-start.1 = ((f32[8,4,3,256]{3,1,2,0:T(4,128)}), f32[8,4,3,256]{3,1,2,0:T(4,128)S(1)}, u32[]{:S(2)}, u32[]{:S(2)}) async-start(f32[8,4,3,256]{3,1,2,0:T(4,128)} %select_bitcast_fusion), calls=%async_computation.1 | async-start | bytes 196608 | tf_op jit(solution)/shard_map/all_to_all | solution.py:118
  341.3 127.9 %all-reduce.2.cloned.1.call-start = ((), (), s32[]{:S(2)}) async-start(), calls=%async_computation.3 | async-start | bytes 1048576 | tf_op jit(solution)/shard_map/psum | solution.py:130
  347.2 9.2 %copy-start.1 = (f32[32,128,256]{2,1,0:T(8,128)S(1)}, f32[32,128,256]{2,1,0:T(8,128)}, u32[]{:S(2)}) copy-start(f32[32,128,256]{2,1,0:T(8,128)} %param.24) | copy-start | bytes 12582916
Sparse Core Ops, SparseCore 0:
  431.3 37.8 all-reduce.1
